TPU v7x, 32 devices: a whole 2x2x4 slice. The times are simulated.
32 devices in a mesh: groups: 2 (over x), ctx: 16 (over z, y, core).
Axes of the slice: x: 2, y: 2, z: 4, core: 2. Of those that a mesh axis runs over, the one named last changes fastest.
Arguments:
- queries: bfloat16 [4096, 2048], P(('groups', 'ctx')), parts along dimension 0, may hold values from -6 to 6
- keys: bfloat16 [4096, 2048], P(('groups', 'ctx')), parts along dimension 0, may hold values from -6 to 6
- values: bfloat16 [4096, 2048], P(('groups', 'ctx')), parts along dimension 0, may hold values from -6 to 6
- out_grad: bfloat16 [4096, 2048], P(('groups', 'ctx')), parts along dimension 0, may hold values from -6 to 6
- conv_weight: float32 [8, 16], replicated, may hold values from -2 to 2
Outputs:
- dq: bfloat16 [4096, 2048], P(('groups', 'ctx')), parts along dimension 0
- dk: bfloat16 [4096, 2048], P(('groups', 'ctx')), parts along dimension 0
- dv: bfloat16 [4096, 2048], P(('groups', 'ctx')), parts along dimension 0
- dconv: float32 [16, 16], P('groups'), parts along dimension 0
There are 2 independent parts, one for each index of `groups`. A program takes and returns all parts, laid end to end along the dimension named above; an argument that names none is the same for every part. Nothing has to cross between parts.
All inputs are finite; a program needn't handle non-finite values.
Results may differ from a plain program's by a relative error of at most 0.024.
Values may be sent and summed in bfloat16 or wider, within the bound.
A program may use at most 128 MiB of HBM per device.

v0:
```python
import jax
import jax.numpy as jnp
from jax import lax
from jax.sharding import PartitionSpec as P


def compress(rows, conv_weight):
    count = rows.shape[0]
    stride, heads = conv_weight.shape
    shaped = rows.reshape(count // stride, stride, heads, -1).astype(jnp.float32)
    merged = jnp.einsum("cshd,sh->chd", shaped, conv_weight).astype(jnp.bfloat16)
    return merged.reshape(count // stride, -1)


def local(queries, keys, values, out_grad, conv_weight):
    count, width = queries.shape
    stride, heads = conv_weight.shape
    head_dim = width // heads
    rows_mem = count // stride
    scale = head_dim ** (-0.5)
    shard_id = lax.axis_index("ctx")
    total_mem = rows_mem * lax.axis_size("ctx")
    q3 = queries.reshape(count, heads, head_dim)
    k3 = keys.reshape(count, heads, head_dim)
    v3 = values.reshape(count, heads, head_dim)
    g3 = out_grad.reshape(count, heads, head_dim)
    mem_keys = compress(keys, conv_weight)
    mem_vals = compress(values, conv_weight)
    causal = jnp.arange(count)[:, None] >= jnp.arange(count)[None, :]
    local_scores = jnp.einsum("shd,thd->hst", q3, k3, preferred_element_type=jnp.float32) * scale
    local_scores = jnp.where(causal[None], local_scores, -1e30)
    high0 = local_scores.max(-1)
    local_prob = jnp.where(causal[None], jnp.exp(local_scores - high0[..., None]), 0.0)
    total0 = local_prob.sum(-1)
    accum0 = jnp.einsum("hst,thd->hsd", local_prob, v3.astype(jnp.float32))

    def score_block(block_keys):
        rows = block_keys.shape[0]
        keys_block = block_keys.reshape(rows, heads, head_dim)
        valid = jnp.arange(rows, dtype=jnp.int32) // rows_mem < shard_id
        scores = (
            jnp.einsum("shd,nhd->hsn", q3, keys_block, preferred_element_type=jnp.float32) * scale
        )
        return (valid, scores)

    all_keys, all_vals = (
        lax.all_gather(mem_keys, "ctx", axis=0, tiled=True),
        lax.all_gather(mem_vals, "ctx", axis=0, tiled=True),
    )
    high = high0
    total = total0
    accum = accum0
    rows = all_keys.shape[0]
    valid, scores = score_block(all_keys)
    scores = jnp.where(valid[None, None, :], scores, -1e30)
    new_high = jnp.maximum(high, scores.max(-1))
    prob = jnp.where(valid[None, None, :], jnp.exp(scores - new_high[..., None]), 0.0)
    factor = jnp.exp(high - new_high)
    vals_block = all_vals.reshape(rows, heads, head_dim)
    total = total * factor + prob.sum(-1)
    accum = accum * factor[..., None] + jnp.einsum(
        "hsn,nhd->hsd", prob, vals_block, preferred_element_type=jnp.float32
    )
    stats = (new_high, total, accum)
    high, total, accum = stats
    lse = high + jnp.log(total)
    output = accum / total[..., None]
    dsum = jnp.einsum("hsd,shd->hs", output, g3.astype(jnp.float32))
    valid_all, scores_all = score_block(all_keys)
    mem_prob = jnp.where(valid_all[None, None, :], jnp.exp(scores_all - lse[..., None]), 0.0)
    keys_all = all_keys.reshape(total_mem, heads, head_dim)
    vals_all = all_vals.reshape(total_mem, heads, head_dim)
    mem_dprob = jnp.einsum("shd,nhd->hsn", g3, vals_all, preferred_element_type=jnp.float32)
    mem_ds = (mem_prob * (mem_dprob - dsum[..., None])).astype(jnp.bfloat16)
    mem_pb = mem_prob.astype(jnp.bfloat16)
    dq_mem = jnp.einsum("hsn,nhd->shd", mem_ds, keys_all, preferred_element_type=jnp.float32)
    dk_part = jnp.einsum("hsn,shd->nhd", mem_ds, q3, preferred_element_type=jnp.float32) * scale
    dv_part = jnp.einsum("hsn,shd->nhd", mem_pb, g3, preferred_element_type=jnp.float32)
    summed = lax.psum_scatter(
        jnp.concatenate(
            (dk_part.reshape(total_mem, width), dv_part.reshape(total_mem, width)), axis=1
        ),
        "ctx",
        scatter_dimension=0,
        tiled=True,
    )
    dmem_k = summed[:, :width].reshape(rows_mem, heads, head_dim)
    dmem_v = summed[:, width:].reshape(rows_mem, heads, head_dim)
    local_p = jnp.where(causal[None], jnp.exp(local_scores - lse[..., None]), 0.0)
    local_dp = jnp.einsum("shd,thd->hst", g3, v3, preferred_element_type=jnp.float32)
    local_ds = (local_p * (local_dp - dsum[..., None])).astype(jnp.bfloat16)
    dq_all = (
        dq_mem + jnp.einsum("hst,thd->shd", local_ds, k3, preferred_element_type=jnp.float32)
    ) * scale
    dk_local = jnp.einsum("hst,shd->thd", local_ds, q3, preferred_element_type=jnp.float32) * scale
    dv_local = jnp.einsum(
        "hst,shd->thd", local_p.astype(jnp.bfloat16), g3, preferred_element_type=jnp.float32
    )
    spread_k = jnp.einsum("chd,sh->cshd", dmem_k, conv_weight).reshape(count, heads, head_dim)
    spread_v = jnp.einsum("chd,sh->cshd", dmem_v, conv_weight).reshape(count, heads, head_dim)
    dq = dq_all.reshape(count, width).astype(jnp.bfloat16)
    dk = (dk_local + spread_k).reshape(count, width).astype(jnp.bfloat16)
    dv = (dv_local + spread_v).reshape(count, width).astype(jnp.bfloat16)
    key_rows = keys.reshape(rows_mem, stride, heads, head_dim).astype(jnp.float32)
    val_rows = values.reshape(rows_mem, stride, heads, head_dim).astype(jnp.float32)
    partial_conv = jnp.einsum("chd,cshd->sh", dmem_k, key_rows) + jnp.einsum(
        "chd,cshd->sh", dmem_v, val_rows
    )
    dconv = lax.psum(partial_conv, "ctx")
    return (dq, dk, dv, dconv)


def solution(mesh):
    return jax.shard_map(
        local,
        mesh=mesh,
        in_specs=(
            P(("groups", "ctx"), None),
            P(("groups", "ctx"), None),
            P(("groups", "ctx"), None),
            P(("groups", "ctx"), None),
            P(),
        ),
        out_specs=(
            P(("groups", "ctx"), None),
            P(("groups", "ctx"), None),
            P(("groups", "ctx"), None),
            P("groups", None),
        ),
        check_vma=False,
    )
```

profile of v0, /device:TPU:0, one launch (start us, length us, event | category | flops | bytes accessed | tf_op | source)
XLA Modules:
  0.0 238.7 jit_solution(13422166051931242764)
XLA Ops:
  8.1 1.4 fusion.38
  10.2 1.3 fusion.36
  13.0 1.2 copy.80
  15.9 35.5 %all-gather.3.cloned.1.call-done = bf16[256,2048]{1,0:T(8,128)(2,1)} async-done(((bf16[16,2048]{1,0:T(8,128)(2,1)}), bf16[256,2048]{1,0:T(8,128)(2,1)}) %all-gather.3.cloned.1.call-update) | async-done | bytes 1048592 | tf_op jit(solution)/shard_map/all_gather | solution.py:47
  51.4 2.3 copy.58
  53.6 1.8 bitcast_reduce_fusion
  56.1 34.3 %all-gather.5.cloned.1.call-done = bf16[256,2048]{1,0:T(8,128)(2,1)} async-done(((bf16[16,2048]{1,0:T(8,128)(2,1)}), bf16[256,2048]{1,0:T(8,128)(2,1)}) %all-gather.5.cloned.1.call-update) | async-done | bytes 1048592 | tf_op jit(solution)/shard_map/all_gather | solution.py:48
  90.4 2.3 copy.63
  92.7 2.2 fusion.3
  96.5 3.1 %fusion.19 = f32[16,256,128]{1,2,0:T(8,128)} fusion(bf16[128,16,128]{0,2,1:T(8,128)(2,1)} %copy.80, f32[16,256,128]{2,1,0:T(8,128)S(1)} %get-tuple-element.26, f32[16,128]{1,0:T(8,128)S(1)} %get-tuple-element.16, pred[256]{0:T(512)(128)(4,1)S(1)} %fusion.48), kind=kOutput, calls=%fused_computation.31 | convolution fusion | flops 136314880 | bytes 4727040 | tf_op jit(solution)/shard_map/hsn,shd->nhd/dot_general | solution.py:78
  101.9 1.8 copy.79
  103.7 4.5 %pad_maximum_fusion = f32[256,4096]{0,1:T(8,128)} fusion(f32[256,2048]{0,1:T(8,128)} %bitcast.140, f32[256,2048]{0,1:T(8,128)} %bitcast.141), kind=kLoop, calls=%fused_computation | loop fusion | flops 1048576 | bytes 8388608 | tf_op jit(solution)/shard_map/concatenate | solution.py:80
  108.2 5.6 %copy.125 = f32[256,4096]{1,0:T(8,128)} copy(f32[256,4096]{0,1:T(8,128)} %pad_maximum_fusion) | data formatting | bytes 8388608
  113.8 1.2 copy-done.2
  115.0 1.6 fusion.17
  119.3 66.5 %reduce-scatter.4.cloned.1.call-done = f32[16,4096]{1,0:T(8,128)} async-done(((f32[256,4096]{1,0:T(8,128)}), f32[16,4096]{1,0:T(8,128)}) %reduce-scatter.4.cloned.1.call-update) | async-done | bytes 262160
  187.8 1.3 multiply_reduce_fusion
  191.6 30.1 %psum.7 = f32[8,16]{1,0:T(8,128)} all-reduce(f32[8,16]{1,0:T(8,128)S(1)} %add_bitcast_fusion), channel_id=1, replica_groups=mesh['groups'=2,'ctx'=16] {'ctx'}, use_global_device_ids=true, to_apply=%region_5.6 | all-reduce | flops 128 | bytes 1024 | tf_op jit(solution)/shard_map/psum | solution.py:109
  221.7 2.4 broadcast_multiply_fusion
  224.1 1.6 copy.86
  225.7 1.3 fusion.18
  227.0 2.1 copy.89
  229.1 1.6 copy.82
  231.2 1.0 copy.88
  (80 shorter events, 16.8 us)
Async XLA Ops:
  7.2 5.2 %copy-start.4 = (bf16[128,2048]{1,0:T(8,128)(2,1)S(1)}, bf16[128,2048]{1,0:T(8,128)(2,1)}, u32[]{:S(2)}) copy-start(bf16[128,2048]{1,0:T(8,128)(2,1)} %param.6) | copy-start | bytes 1572868
  7.2 5.5 %copy-start.16 = (bf16[128,2048]{1,0:T(8,128)(2,1)S(1)}, bf16[128,2048]{1,0:T(8,128)(2,1)}, u32[]{:S(2)}) copy-start(bf16[128,2048]{1,0:T(8,128)(2,1)} %param.5) | copy-start | bytes 1572868
  7.2 44.2 %all-gather.3.cloned.1.call-start = ((), (), s32[]{:S(2)}) async-start(), calls=%async_computation.1 | async-start | bytes 1114112 | tf_op jit(solution)/shard_map/all_gather | solution.py:47
  8.1 4.8 %copy-start.17 = (bf16[128,2048]{1,0:T(8,128)(2,1)S(1)}, bf16[128,2048]{1,0:T(8,128)(2,1)}, u32[]{:S(2)}) copy-start(bf16[128,2048]{1,0:T(8,128)(2,1)} %param.8) | copy-start | bytes 1572868
  10.2 80.2 %all-gather.5.cloned.1.call-start = ((), (), s32[]{:S(2)}) async-start(), calls=%async_computation.2 | async-start | bytes 1114112 | tf_op jit(solution)/shard_map/all_gather | solution.py:48
  12.3 173.5 %reduce-scatter.4.cloned.1.call-start = ((), (), s32[]{:S(2)}) async-start(), calls=%async_computation.3 | async-start | bytes 4456448
  12.6 2.1 copy-start.8
  14.7 1.0 copy-start
  92.7 2.2 copy-start.1
  92.7 2.2 copy-start.14
  94.9 19.0 %copy-start.18 = (f32[16,128]{1,0:T(8,128)}, f32[16,128]{1,0:T(8,128)S(1)}, u32[]{:S(2)}) copy-start(f32[16,128]{1,0:T(8,128)S(1)} %get-tuple-element.16) | copy-start | bytes 24580
  96.5 3.1 %copy-start.6 = (bf16[128,16,128]{0,2,1:T(8,128)(2,1)S(1)}, bf16[128,16,128]{0,2,1:T(8,128)(2,1)}, u32[]{:S(2)}) copy-start(bf16[128,16,128]{0,2,1:T(8,128)(2,1)} %copy.80) | copy-start | bytes 1572868
  96.5 3.1 %copy-start.15 = (bf16[256,2048]{0,1:T(8,128)(2,1)S(1)}, bf16[256,2048]{0,1:T(8,128)(2,1)}, u32[]{:S(2)}) copy-start(bf16[256,2048]{0,1:T(8,128)(2,1)} %copy.63) | copy-start | bytes 3145732
  100.5 1.0 copy-start.10
  113.8 1.2 copy-start.2
  115.0 1.6 copy-start.3
  115.0 1.7 copy-start.11
  116.7 1.5 copy-start.12
  116.7 1.2 copy-start.9
  187.7 2.9 %copy-start.5 = (bf16[128,2048]{1,0:T(8,128)(2,1)S(1)}, bf16[128,2048]{1,0:T(8,128)(2,1)}, u32[]{:S(2)}) copy-start(bf16[128,2048]{1,0:T(8,128)(2,1)} %param.6) | copy-start | bytes 1572868
  221.7 4.0 %copy-start.7 = (bf16[128,16,128]{0,2,1:T(8,128)(2,1)S(1)}, bf16[128,16,128]{0,2,1:T(8,128)(2,1)}, u32[]{:S(2)}) copy-start(bf16[128,16,128]{0,2,1:T(8,128)(2,1)} %copy.80) | copy-start | bytes 1572868
  221.7 4.0 %copy-start.19 = (f32[16,128]{1,0:T(8,128)S(1)}, f32[16,128]{1,0:T(8,128)}, u32[]{:S(2)}) copy-start(f32[16,128]{1,0:T(8,128)} %copy-done.18) | copy-start | bytes 24580
  227.0 3.7 %copy-start.13 = (bf16[16,128,128]{1,2,0:T(8,128)(2,1)S(1)}, bf16[16,128,128]{1,2,0:T(8,128)(2,1)}, u32[]{:S(2)}) copy-start(bf16[16,128,128]{1,2,0:T(8,128)(2,1)} %copy-done.12) | copy-start | bytes 1572868
Sparse Core Ops, SparseCore 0:
  10.7 40.5 all-gather.2
  53.5 36.8 all-gather.4
  114.0 71.7 reduce-scatter.3
where the time goes:
time: 239 us
  waiting for transfers between devices  136 us (57%)
  local copies, waits for them, and re-layouts  31.1 us (13%)
  blocking collectives  30.1 us (13%)
  matrix products  16.4 us (7%)
  between operations  14.1 us (6%)
  other arithmetic  10.6 us (4%)
    unnamed x4, waiting for transfers between devices  66.5 us
    all_gather x1, waiting for transfers between devices, local(): lax.all_gather(mem_keys, 'ctx', axis=0, tiled=True)  35.5 us
    all_gather x1, waiting for transfers between devices, local(): lax.all_gather(mem_vals, 'ctx', axis=0, tiled=True)  34.3 us
    psum x1, blocking collectives, local(): dconv = lax.psum(partial_conv, 'ctx')  30.1 us
    unnamed x52, local copies, waits for them, and re-layouts  17.3 us
  transfers between devices with their start and end apart: 3, of which 3 were waited for; matrix products, arithmetic and copies ran while one was open for 5% of the time, Pallas kernels for 0%

commit v1 on v0

v1 whole, which is shorter than its diff:
```python
import functools

import jax
import jax.numpy as jnp
from jax import lax
from jax.experimental import pallas as pl
from jax.experimental.pallas import tpu as pltpu
from jax.sharding import PartitionSpec as P

MESH = pl.DeviceIdType.MESH
F32 = jnp.float32
BF16 = jnp.bfloat16
LAYER = 4
HEADS_PER_STEP = 2


def dot(a, b, ca, cb):
    return lax.dot_general(a, b, (((ca,), (cb,)), ((), ())), preferred_element_type=F32)


def kernel(
    n, q_ref, k_ref, v_ref, g_ref, cw_ref, dq_ref, dk_ref, dv_ref, dc_ref,
    mem, part, cbuf, ybuf, zbuf, dbuf, wexp, dkl, dvl,
    az_s, az_r, ay_s, ay_r, ac_s, ac_r,
    rc_s, rc_r, ry_s, ry_r, rz_s, rz_r, d_s, d_r,
):
    count, width = q_ref.shape
    stride, heads = cw_ref.shape
    dim = width // heads
    rows = count // stride
    layers = n // LAYER
    total = rows * n
    scale = dim ** (-0.5)
    me = lax.axis_index("ctx")
    z = me // LAYER
    r = me % LAYER
    y = r // 2
    c = r % 2
    base = z * LAYER
    core_peer = base + y * 2 + (1 - c)
    y_peer = base + (1 - y) * 2 + c

    barrier = pltpu.get_barrier_semaphore()

    def greet(i, carry):
        pl.semaphore_signal(
            barrier, inc=1, device_id={"ctx": (me + i) % n}, device_id_type=MESH
        )
        return carry

    lax.fori_loop(1, n, greet, 0)

    def block(ref, owner):
        return ref.at[:, pl.ds(pl.multiple_of(owner * rows, rows), rows), :]

    def lanes(h):
        return pl.ds(pl.multiple_of(h * dim, dim), dim)

    def remote(src, dst, send, recv, dev):
        return pltpu.make_async_remote_copy(
            src_ref=src, dst_ref=dst, send_sem=send, recv_sem=recv,
            device_id={"ctx": dev}, device_id_type=MESH,
        )

    for h in range(heads):
        wexp[:, h * dim:(h + 1) * dim] = jnp.broadcast_to(cw_ref[:, h:h + 1], (stride, dim))

    my_rows = pl.ds(pl.multiple_of(me * rows, rows), rows)

    def compress(h, carry):
        w = wexp[:, lanes(h)][None]
        for i, src in enumerate((k_ref, v_ref)):
            x = src[:, lanes(h)].astype(F32).reshape(rows, stride, dim)
            mem[i, my_rows, lanes(h)] = (x * w).sum(axis=1).astype(BF16)
        return carry

    lax.fori_loop(0, heads, compress, 0)
    pl.semaphore_wait(barrier, n - 1)

    def gather_z(to, sender):
        own = block(mem, sender * LAYER + r)
        return remote(own, own, az_s.at[to], az_r.at[sender], to * LAYER + r)

    def gather_y(zs, yy):
        b = block(mem, zs * LAYER + yy * 2 + c)
        return remote(b, b, ay_s.at[zs], ay_r.at[zs], y_peer)

    def gather_c(zs, yy, cc):
        b = block(mem, zs * LAYER + yy * 2 + cc)
        return remote(b, b, ac_s.at[zs, yy], ac_r.at[zs, yy], core_peer)

    def each(lo, hi, fn):
        def step(i, carry):
            fn(i)
            return carry
        lax.fori_loop(lo, hi, step, 0)

    each(0, layers - 1 - z, lambda i: gather_z(layers - 1 - i, z).start())
    gather_y(z, y).start()
    gather_c(z, y, c).start()

    def clear(zs):
        span = pl.ds(pl.multiple_of(zs * LAYER * rows, LAYER * rows), LAYER * rows)
        mem[:, span, :] = jnp.zeros((2, LAYER * rows, width), BF16)

    each(z + 1, layers, clear)

    def arrive_z(i):
        zs = z - i
        gather_z(z, zs).wait_recv()
        gather_y(zs, y).start()
        gather_c(zs, y, c).start()

    def arrive_y(i):
        zs = z - i
        gather_y(zs, 1 - y).wait_recv()
        gather_c(zs, 1 - y, c).start()

    def arrive_c(i):
        zs = z - i
        gather_c(zs, y, 1 - c).wait_recv()
        gather_c(zs, 1 - y, 1 - c).wait_recv()

    each(1, z + 1, arrive_z)
    each(0, z + 1, arrive_y)
    each(0, z + 1, arrive_c)

    valid = lax.broadcasted_iota(jnp.int32, (total, count), 0) < me * rows
    causal = lax.broadcasted_iota(jnp.int32, (count, count), 0) <= lax.broadcasted_iota(
        jnp.int32, (count, count), 1
    )

    def one_head(h):
        q, k, v, g = (x[:, lanes(h)] for x in (q_ref, k_ref, v_ref, g_ref))
        mk, mv = mem[0, :, lanes(h)], mem[1, :, lanes(h)]
        sm = jnp.where(valid, dot(mk, q, 1, 1) * scale, -1e30)
        sl = jnp.where(causal, dot(k, q, 1, 1) * scale, -1e30)
        dpm, dpl = dot(mv, g, 1, 1), dot(v, g, 1, 1)
        high = jnp.maximum(sm.max(0, keepdims=True), sl.max(0, keepdims=True))
        em, el = jnp.exp(sm - high), jnp.exp(sl - high)
        inv = 1.0 / (em.sum(0, keepdims=True) + el.sum(0, keepdims=True))
        pm, plo = em * inv, el * inv
        dsum = (pm * dpm).sum(0, keepdims=True) + (plo * dpl).sum(0, keepdims=True)
        dsm = (pm * (dpm - dsum)).astype(BF16)
        dsl = (plo * (dpl - dsum)).astype(BF16)
        dq = (dot(dsm, mk, 0, 0) + dot(dsl, k, 0, 0)) * scale
        pk = dot(dsm, q, 1, 0) * scale
        pv = dot(pm.astype(BF16), g, 1, 0)
        lk = dot(dsl, q, 1, 0) * scale
        lv = dot(plo.astype(BF16), g, 1, 0)
        return dq.astype(BF16), pk.astype(BF16), pv.astype(BF16), lk, lv

    def head_step(i):
        hs = [i * HEADS_PER_STEP + j for j in range(HEADS_PER_STEP)]
        for h, (dq, pk, pv, lk, lv) in zip(hs, [one_head(h) for h in hs]):
            dq_ref[:, lanes(h)] = dq
            part[0, :, lanes(h)] = pk
            part[1, :, lanes(h)] = pv
            dkl[:, lanes(h)] = lk
            dvl[:, lanes(h)] = lv

    each(0, heads // HEADS_PER_STEP, head_step)

    def reduce_c(zs, yy, cc):
        return remote(
            block(part, zs * LAYER + yy * 2 + cc), cbuf.at[zs * 2 + yy],
            rc_s.at[zs, yy], rc_r.at[zs, yy], core_peer,
        )

    def reduce_y(zs, yy):
        return remote(
            block(part, zs * LAYER + yy * 2 + c), ybuf.at[zs], ry_s.at[zs], ry_r.at[zs], y_peer
        )

    def reduce_z(to, sender):
        return remote(
            block(part, to * LAYER + r), zbuf.at[sender], rz_s.at[to], rz_r.at[sender],
            to * LAYER + r,
        )

    def send_c(zs):
        reduce_c(zs, 1 - y, 1 - c).start()
        reduce_c(zs, y, 1 - c).start()

    each(0, z + 1, send_c)

    def add_into(owner, other):
        b = block(part, owner)
        b[...] = (b[...].astype(F32) + other[...].astype(F32)).astype(BF16)

    def sum_c(zs):
        reduce_c(zs, 1 - y, c).wait_recv()
        add_into(zs * LAYER + (1 - y) * 2 + c, cbuf.at[zs * 2 + 1 - y])
        reduce_y(zs, 1 - y).start()
        reduce_c(zs, y, c).wait_recv()
        add_into(zs * LAYER + r, cbuf.at[zs * 2 + y])

    each(0, z + 1, sum_c)

    def sum_y(zs):
        reduce_y(zs, y).wait_recv()
        add_into(zs * LAYER + r, ybuf.at[zs])

        @pl.when(zs < z)
        def _():
            reduce_z(zs, z).start()

    each(0, z + 1, sum_y)

    zbuf[z] = part[:, my_rows, :]
    each(z + 1, layers, lambda zz: reduce_z(z, zz).wait_recv())

    def clear_z(zz):
        zbuf[zz] = jnp.zeros((2, rows, width), BF16)

    each(0, z, clear_z)

    lane = lax.broadcasted_iota(jnp.int32, (stride, dbuf.shape[-1]), 1)

    def conv_head(h, acc):
        t = jnp.zeros((stride, dim), F32)
        for i, (src, loc, out) in enumerate(((k_ref, dkl, dk_ref), (v_ref, dvl, dv_ref))):
            x = src[:, lanes(h)].astype(F32).reshape(rows, stride, dim)
            d = zbuf[:, i, :, lanes(h)].astype(F32).sum(axis=0)[:, None, :]
            t += (x * d).sum(axis=0)
            spread = (d * wexp[:, lanes(h)][None]).reshape(count, dim)
            out[:, lanes(h)] = (loc[:, lanes(h)] + spread).astype(BF16)
        return jnp.where(lane == h, t.sum(axis=1, keepdims=True), acc)

    dbuf[me] = lax.fori_loop(0, heads, conv_head, jnp.zeros(lane.shape, F32))

    def conv_copy(to, sender):
        return remote(dbuf.at[sender], dbuf.at[sender], d_s.at[to], d_r.at[sender], to)

    each(1, n, lambda i: conv_copy((me + i) % n, me).start())

    each(z + 1, layers, lambda to: gather_z(to, z).wait_send())

    def ended(zs):
        gather_y(zs, y).wait_send()
        gather_c(zs, y, c).wait_send()
        gather_c(zs, 1 - y, c).wait_send()
        reduce_c(zs, 0, 1 - c).wait_send()
        reduce_c(zs, 1, 1 - c).wait_send()
        reduce_y(zs, 1 - y).wait_send()

    each(0, z + 1, ended)
    each(0, z, lambda zs: reduce_z(zs, z).wait_send())
    each(1, n, lambda i: conv_copy(me, (me + i) % n).wait_recv())
    dc_ref[...] = dbuf[...].sum(axis=0)[:, :heads]
    each(1, n, lambda i: conv_copy((me + i) % n, me).wait_send())


def local(n, queries, keys, values, out_grad, conv_weight):
    count, width = queries.shape
    stride, heads = conv_weight.shape
    rows = count // stride
    layers = n // LAYER
    big = jax.ShapeDtypeStruct((count, width), BF16)
    vmem = pl.BlockSpec(memory_space=pltpu.VMEM)
    dma = pltpu.SemaphoreType.DMA
    return pl.pallas_call(
        functools.partial(kernel, n),
        out_shape=(big, big, big, jax.ShapeDtypeStruct((stride, heads), F32)),
        in_specs=[vmem] * 5,
        out_specs=[vmem] * 4,
        scratch_shapes=[
            pltpu.VMEM((2, rows * n, width), BF16),
            pltpu.VMEM((2, rows * n, width), BF16),
            pltpu.VMEM((layers * 2, 2, rows, width), BF16),
            pltpu.VMEM((layers, 2, rows, width), BF16),
            pltpu.VMEM((layers, 2, rows, width), BF16),
            pltpu.VMEM((n, stride, 128 * pl.cdiv(heads, 128)), F32),
            pltpu.VMEM((stride, width), F32),
            pltpu.VMEM((count, width), F32),
            pltpu.VMEM((count, width), F32),
            dma((layers,)), dma((layers,)), dma((layers,)), dma((layers,)),
            dma((layers, 2)), dma((layers, 2)),
            dma((layers, 2)), dma((layers, 2)),
            dma((layers,)), dma((layers,)), dma((layers,)), dma((layers,)),
            dma((n,)), dma((n,)),
        ],
        compiler_params=pltpu.CompilerParams(
            collective_id=0, has_side_effects=True, vmem_limit_bytes=60 * 2**20
        ),
    )(queries, keys, values, out_grad, conv_weight)


def solution(mesh):
    rows = P(("groups", "ctx"), None)
    return jax.shard_map(
        functools.partial(local, mesh.shape["ctx"]),
        mesh=mesh,
        in_specs=(rows, rows, rows, rows, P()),
        out_specs=(rows, rows, rows, P("groups", None)),
        check_vma=False,
    )
```

time: 239 us -> 65.2 us (0.27)
  waiting for transfers between devices: 136 us -> 0 us
  Pallas kernels: 0 us -> 59.8 us
  blocking collectives: 30.1 us -> 0 us
  local copies, waits for them, and re-layouts: 31.1 us -> 4.56 us
  matrix products: 16.4 us -> 0 us
  between operations: 14.1 us -> 0.65 us
  other arithmetic: 10.6 us -> 0 us
    all_gather x2 -> x0, waiting for transfers between devices: 69.8 us -> none  [the longest x1 35.5 us: local(): lax.all_gather(mem_keys, 'ctx', axis=0, tiled=True)]
    unnamed x4 -> x0, waiting for transfers between devices: 66.5 us -> none
    pallas_call x0 -> x1, Pallas kernels: none -> 59.8 us  [local(): pl.pallas_call(functools.partial(kernel, n), out_shape=(big, big, big, ja...]
    psum x1 -> x0, blocking collectives: 30.1 us -> none  [local(): dconv = lax.psum(partial_conv, 'ctx')]
    dot_general x14 -> x0, matrix products: 16.4 us -> none  [the longest x1 3.07 us: local(): jnp.einsum('hsn,shd->nhd', mem_pb, g3, preferred_element_type=jnp.float32)]
    unnamed x52 -> x10, local copies, waits for them, and re-layouts: 17.3 us -> 4.56 us
    reshape x7 -> x0, local copies, waits for them, and re-layouts: 5.55 us -> none  [the longest x1 1.58 us: local(): jnp.einsum('chd,sh->cshd', dmem_k, conv_weight)]
    all_gather x2 -> x0, local copies, waits for them, and re-layouts: 4.57 us -> none  [the longest x1 2.3 us: local(): lax.all_gather(mem_keys, 'ctx', axis=0, tiled=True)]
  transfers between devices with their start and end apart: 3 -> 0, of which waited for: 3 -> 0; matrix products, arithmetic and copies ran while one was open for 5% -> 0% of each run, Pallas kernels for 0% -> 0%
where the time goes in v1:
time: 65.2 us; the launch traced here: 65 us
  Pallas kernels  59.8 us (92%)
  local copies, waits for them, and re-layouts  4.56 us (7%)
    pallas_call x1, Pallas kernels, local(): pl.pallas_call(functools.partial(kernel, n), out_shape=(big, big, big, ja...  59.8 us
    unnamed x10, local copies, waits for them, and re-layouts  4.56 us

profile of v1, /device:TPU:0, one launch (start us, length us, event | category | flops | bytes accessed | tf_op | source)
XLA Modules:
  0.0 65.0 jit_solution(10232619152939544980)
XLA Ops:
  0.6 59.8 %shard_map.84 = (bf16[128,2048]{1,0:T(8,128)(2,1)}, bf16[128,2048]{1,0:T(8,128)(2,1)}, bf16[128,2048]{1,0:T(8,128)(2,1)}, f32[8,16]{1,0:T(8,128)}) custom-call(bf16[128,2048]{1,0:T(8,128)(2,1)} %q_ref.1, bf16[128,2048]{1,0:T(8,128)(2,1)} %k_ref.1, bf16[128,2048]{1,0:T(8,128)(2,1)} %v_ref.1, bf16[128,2048]{1,0:T(8,128)(2,1)} %g_ref.1, f32[8,16]{1,0:T(8,128)} %cw_ref.1), custom_call_target="tpu_custom_call" | custom-call | tf_op jit(solution)/shard_map/pallas_call | solution.py:262
  60.4 0.0 copy-start.1
  60.5 1.9 %copy.13 = bf16[128,2048]{1,0:T(8,128)(2,1)} copy(bf16[128,2048]{1,0:T(8,128)(2,1)} %get-tuple-element.8) | data formatting | bytes 1048576
  62.4 0.0 copy-done.1
  62.4 0.0 copy-start
  62.4 0.8 %copy.14 = bf16[128,2048]{1,0:T(8,128)(2,1)} copy(bf16[128,2048]{1,0:T(8,128)(2,1)S(1)} %copy-done.1) | data formatting | bytes 1048576
  63.2 0.4 copy-done
  63.6 0.0 copy-start.2
  63.6 0.8 %copy.15 = bf16[128,2048]{1,0:T(8,128)(2,1)} copy(bf16[128,2048]{1,0:T(8,128)(2,1)S(1)} %copy-done) | data formatting | bytes 1048576
  64.4 0.0 copy-done.2
  64.4 0.6 copy.16
Async XLA Ops:
  60.4 2.0 %copy-start.1 = (bf16[128,2048]{1,0:T(8,128)(2,1)S(1)}, bf16[128,2048]{1,0:T(8,128)(2,1)}, u32[]{:S(2)}) copy-start(bf16[128,2048]{1,0:T(8,128)(2,1)} %get-tuple-element.9) | copy-start | bytes 1572868
  62.4 1.2 %copy-start = (bf16[128,2048]{1,0:T(8,128)(2,1)S(1)}, bf16[128,2048]{1,0:T(8,128)(2,1)}, u32[]{:S(2)}) copy-start(bf16[128,2048]{1,0:T(8,128)(2,1)} %get-tuple-element.10) | copy-start | bytes 1572868
  63.6 0.8 %copy-start.2 = (f32[8,16]{1,0:T(8,128)S(1)}, f32[8,16]{1,0:T(8,128)}, u32[]{:S(2)}) copy-start(f32[8,16]{1,0:T(8,128)} %get-tuple-element.11) | copy-start | bytes 1540

commit v2 on v1

--- a/solution.py
+++ b/solution.py
@@ -12,6 +12,7 @@
 BF16 = jnp.bfloat16
 LAYER = 4
 HEADS_PER_STEP = 2
+GROUPS = 4
 
 
 def dot(a, b, ca, cb):
@@ -50,8 +51,13 @@
 
     lax.fori_loop(1, n, greet, 0)
 
-    def block(ref, owner):
-        return ref.at[:, pl.ds(pl.multiple_of(owner * rows, rows), rows), :]
+    part_width = width // GROUPS
+
+    def cols(gi):
+        return pl.ds(gi * part_width, part_width)
+
+    def block(ref, owner, gi):
+        return ref.at[:, pl.ds(pl.multiple_of(owner * rows, rows), rows), cols(gi)]
 
     def lanes(h):
         return pl.ds(pl.multiple_of(h * dim, dim), dim)
@@ -77,17 +83,17 @@
     lax.fori_loop(0, heads, compress, 0)
     pl.semaphore_wait(barrier, n - 1)
 
-    def gather_z(to, sender):
-        own = block(mem, sender * LAYER + r)
-        return remote(own, own, az_s.at[to], az_r.at[sender], to * LAYER + r)
-
-    def gather_y(zs, yy):
-        b = block(mem, zs * LAYER + yy * 2 + c)
-        return remote(b, b, ay_s.at[zs], ay_r.at[zs], y_peer)
-
-    def gather_c(zs, yy, cc):
-        b = block(mem, zs * LAYER + yy * 2 + cc)
-        return remote(b, b, ac_s.at[zs, yy], ac_r.at[zs, yy], core_peer)
+    def gather_z(gi, to, sender):
+        own = block(mem, sender * LAYER + r, gi)
+        return remote(own, own, az_s.at[gi, to], az_r.at[gi, sender], to * LAYER + r)
+
+    def gather_y(gi, zs, yy):
+        b = block(mem, zs * LAYER + yy * 2 + c, gi)
+        return remote(b, b, ay_s.at[gi, zs], ay_r.at[gi, zs], y_peer)
+
+    def gather_c(gi, zs, yy, cc):
+        b = block(mem, zs * LAYER + yy * 2 + cc, gi)
+        return remote(b, b, ac_s.at[gi, zs, yy], ac_r.at[gi, zs, yy], core_peer)
 
     def each(lo, hi, fn):
         def step(i, carry):
@@ -95,9 +101,10 @@
             return carry
         lax.fori_loop(lo, hi, step, 0)
 
-    each(0, layers - 1 - z, lambda i: gather_z(layers - 1 - i, z).start())
-    gather_y(z, y).start()
-    gather_c(z, y, c).start()
+    for gi in range(GROUPS):
+        each(0, layers - 1 - z, lambda i: gather_z(gi, layers - 1 - i, z).start())
+        gather_y(gi, z, y).start()
+        gather_c(gi, z, y, c).start()
 
     def clear(zs):
         span = pl.ds(pl.multiple_of(zs * LAYER * rows, LAYER * rows), LAYER * rows)
@@ -105,25 +112,21 @@
 
     each(z + 1, layers, clear)
 
-    def arrive_z(i):
+    def arrive_z(gi, i):
         zs = z - i
-        gather_z(z, zs).wait_recv()
-        gather_y(zs, y).start()
-        gather_c(zs, y, c).start()
-
-    def arrive_y(i):
+        gather_z(gi, z, zs).wait_recv()
+        gather_y(gi, zs, y).start()
+        gather_c(gi, zs, y, c).start()
+
+    def arrive_y(gi, i):
         zs = z - i
-        gather_y(zs, 1 - y).wait_recv()
-        gather_c(zs, 1 - y, c).start()
-
-    def arrive_c(i):
+        gather_y(gi, zs, 1 - y).wait_recv()
+        gather_c(gi, zs, 1 - y, c).start()
+
+    def arrive_c(gi, i):
         zs = z - i
-        gather_c(zs, y, 1 - c).wait_recv()
-        gather_c(zs, 1 - y, 1 - c).wait_recv()
-
-    each(1, z + 1, arrive_z)
-    each(0, z + 1, arrive_y)
-    each(0, z + 1, arrive_c)
+        gather_c(gi, zs, y, 1 - c).wait_recv()
+        gather_c(gi, zs, 1 - y, 1 - c).wait_recv()
 
     valid = lax.broadcasted_iota(jnp.int32, (total, count), 0) < me * rows
     causal = lax.broadcasted_iota(jnp.int32, (count, count), 0) <= lax.broadcasted_iota(
@@ -159,56 +162,66 @@
             dkl[:, lanes(h)] = lk
             dvl[:, lanes(h)] = lv
 
-    each(0, heads // HEADS_PER_STEP, head_step)
-
-    def reduce_c(zs, yy, cc):
+    steps = heads // HEADS_PER_STEP // GROUPS
+
+    def reduce_c(gi, zs, yy, cc):
         return remote(
-            block(part, zs * LAYER + yy * 2 + cc), cbuf.at[zs * 2 + yy],
-            rc_s.at[zs, yy], rc_r.at[zs, yy], core_peer,
-        )
-
-    def reduce_y(zs, yy):
+            block(part, zs * LAYER + yy * 2 + cc, gi), cbuf.at[zs * 2 + yy, :, :, cols(gi)],
+            rc_s.at[gi, zs, yy], rc_r.at[gi, zs, yy], core_peer,
+        )
+
+    def reduce_y(gi, zs, yy):
         return remote(
-            block(part, zs * LAYER + yy * 2 + c), ybuf.at[zs], ry_s.at[zs], ry_r.at[zs], y_peer
-        )
-
-    def reduce_z(to, sender):
+            block(part, zs * LAYER + yy * 2 + c, gi), ybuf.at[zs, :, :, cols(gi)],
+            ry_s.at[gi, zs], ry_r.at[gi, zs], y_peer,
+        )
+
+    def reduce_z(gi, to, sender):
         return remote(
-            block(part, to * LAYER + r), zbuf.at[sender], rz_s.at[to], rz_r.at[sender],
-            to * LAYER + r,
-        )
-
-    def send_c(zs):
-        reduce_c(zs, 1 - y, 1 - c).start()
-        reduce_c(zs, y, 1 - c).start()
-
-    each(0, z + 1, send_c)
-
-    def add_into(owner, other):
-        b = block(part, owner)
+            block(part, to * LAYER + r, gi), zbuf.at[sender, :, :, cols(gi)],
+            rz_s.at[gi, to], rz_r.at[gi, sender], to * LAYER + r,
+        )
+
+    def send_c(gi, zs):
+        reduce_c(gi, zs, 1 - y, 1 - c).start()
+        reduce_c(gi, zs, y, 1 - c).start()
+
+    def add_into(gi, owner, other):
+        b = block(part, owner, gi)
         b[...] = (b[...].astype(F32) + other[...].astype(F32)).astype(BF16)
 
-    def sum_c(zs):
-        reduce_c(zs, 1 - y, c).wait_recv()
-        add_into(zs * LAYER + (1 - y) * 2 + c, cbuf.at[zs * 2 + 1 - y])
-        reduce_y(zs, 1 - y).start()
-        reduce_c(zs, y, c).wait_recv()
-        add_into(zs * LAYER + r, cbuf.at[zs * 2 + y])
-
-    each(0, z + 1, sum_c)
-
-    def sum_y(zs):
-        reduce_y(zs, y).wait_recv()
-        add_into(zs * LAYER + r, ybuf.at[zs])
+    def sum_c(gi, zs):
+        reduce_c(gi, zs, 1 - y, c).wait_recv()
+        add_into(gi, zs * LAYER + (1 - y) * 2 + c, cbuf.at[zs * 2 + 1 - y, :, :, cols(gi)])
+        reduce_y(gi, zs, 1 - y).start()
+        reduce_c(gi, zs, y, c).wait_recv()
+        add_into(gi, zs * LAYER + r, cbuf.at[zs * 2 + y, :, :, cols(gi)])
+
+    def sum_y(gi, zs):
+        reduce_y(gi, zs, y).wait_recv()
+        add_into(gi, zs * LAYER + r, ybuf.at[zs, :, :, cols(gi)])
 
         @pl.when(zs < z)
         def _():
-            reduce_z(zs, z).start()
-
-    each(0, z + 1, sum_y)
+            reduce_z(gi, zs, z).start()
+
+    for s in range(GROUPS + 4):
+        if s < GROUPS:
+            each(1, z + 1, functools.partial(arrive_z, s))
+        if 0 <= s - 1 < GROUPS:
+            each(0, z + 1, functools.partial(arrive_y, s - 1))
+        if 0 <= s - 2 < GROUPS:
+            each(0, z + 1, functools.partial(arrive_c, s - 2))
+            each((s - 2) * steps, (s - 1) * steps, head_step)
+            each(0, z + 1, functools.partial(send_c, s - 2))
+        if 0 <= s - 3 < GROUPS:
+            each(0, z + 1, functools.partial(sum_c, s - 3))
+        if 0 <= s - 4 < GROUPS:
+            each(0, z + 1, functools.partial(sum_y, s - 4))
 
     zbuf[z] = part[:, my_rows, :]
-    each(z + 1, layers, lambda zz: reduce_z(z, zz).wait_recv())
+    for gi in range(GROUPS):
+        each(z + 1, layers, lambda zz: reduce_z(gi, z, zz).wait_recv())
 
     def clear_z(zz):
         zbuf[zz] = jnp.zeros((2, rows, width), BF16)
@@ -234,18 +247,18 @@
 
     each(1, n, lambda i: conv_copy((me + i) % n, me).start())
 
-    each(z + 1, layers, lambda to: gather_z(to, z).wait_send())
-
-    def ended(zs):
-        gather_y(zs, y).wait_send()
-        gather_c(zs, y, c).wait_send()
-        gather_c(zs, 1 - y, c).wait_send()
-        reduce_c(zs, 0, 1 - c).wait_send()
-        reduce_c(zs, 1, 1 - c).wait_send()
-        reduce_y(zs, 1 - y).wait_send()
-
-    each(0, z + 1, ended)
-    each(0, z, lambda zs: reduce_z(zs, z).wait_send())
+    def ended(gi, zs):
+        gather_y(gi, zs, y).wait_send()
+        gather_c(gi, zs, y, c).wait_send()
+        gather_c(gi, zs, 1 - y, c).wait_send()
+        reduce_c(gi, zs, 0, 1 - c).wait_send()
+        reduce_c(gi, zs, 1, 1 - c).wait_send()
+        reduce_y(gi, zs, 1 - y).wait_send()
+
+    for gi in range(GROUPS):
+        each(z + 1, layers, lambda to: gather_z(gi, to, z).wait_send())
+        each(0, z + 1, functools.partial(ended, gi))
+        each(0, z, lambda zs: reduce_z(gi, zs, z).wait_send())
     each(1, n, lambda i: conv_copy(me, (me + i) % n).wait_recv())
     dc_ref[...] = dbuf[...].sum(axis=0)[:, :heads]
     each(1, n, lambda i: conv_copy((me + i) % n, me).wait_send())
@@ -274,10 +287,10 @@
             pltpu.VMEM((stride, width), F32),
             pltpu.VMEM((count, width), F32),
             pltpu.VMEM((count, width), F32),
-            dma((layers,)), dma((layers,)), dma((layers,)), dma((layers,)),
-            dma((layers, 2)), dma((layers, 2)),
-            dma((layers, 2)), dma((layers, 2)),
-            dma((layers,)), dma((layers,)), dma((layers,)), dma((layers,)),
+            dma((GROUPS, layers,)), dma((GROUPS, layers,)), dma((GROUPS, layers,)), dma((GROUPS, layers,)),
+            dma((GROUPS, layers, 2)), dma((GROUPS, layers, 2)),
+            dma((GROUPS, layers, 2)), dma((GROUPS, layers, 2)),
+            dma((GROUPS, layers,)), dma((GROUPS, layers,)), dma((GROUPS, layers,)), dma((GROUPS, layers,)),
             dma((n,)), dma((n,)),
         ],
         compiler_params=pltpu.CompilerParams(

time: 65.2 us -> 56.6 us (0.87)
  Pallas kernels: 59.8 us -> 51.2 us
    pallas_call x1, Pallas kernels: 59.8 us -> 51.2 us  [local(): pl.pallas_call(functools.partial(kernel, n), out_shape=(big, big, big, ja...]
where the time goes in v2:
time: 56.6 us; the launch traced here: 56.4 us
  Pallas kernels  51.2 us (90%)
  local copies, waits for them, and re-layouts  4.56 us (8%)
  between operations  0.65 us (1%)
    pallas_call x1, Pallas kernels, local(): pl.pallas_call(functools.partial(kernel, n), out_shape=(big, big, big, ja...  51.2 us
    unnamed x10, local copies, waits for them, and re-layouts  4.56 us

profile of v2, /device:TPU:0, one launch (start us, length us, event | category | flops | bytes accessed | tf_op | source)
XLA Modules:
  0.0 56.4 jit_solution(1981856010455310579)
XLA Ops:
  0.6 51.2 %shard_map.84 = (bf16[128,2048]{1,0:T(8,128)(2,1)}, bf16[128,2048]{1,0:T(8,128)(2,1)}, bf16[128,2048]{1,0:T(8,128)(2,1)}, f32[8,16]{1,0:T(8,128)}) custom-call(bf16[128,2048]{1,0:T(8,128)(2,1)} %q_ref.1, bf16[128,2048]{1,0:T(8,128)(2,1)} %k_ref.1, bf16[128,2048]{1,0:T(8,128)(2,1)} %v_ref.1, bf16[128,2048]{1,0:T(8,128)(2,1)} %g_ref.1, f32[8,16]{1,0:T(8,128)} %cw_ref.1), custom_call_target="tpu_custom_call" | custom-call | tf_op jit(solution)/shard_map/pallas_call | solution.py:275
  51.8 0.0 copy-start.1
  51.8 1.9 %copy.13 = bf16[128,2048]{1,0:T(8,128)(2,1)} copy(bf16[128,2048]{1,0:T(8,128)(2,1)} %get-tuple-element.8) | data formatting | bytes 1048576
  53.8 0.0 copy-done.1
  53.8 0.0 copy-start
  53.8 0.8 %copy.14 = bf16[128,2048]{1,0:T(8,128)(2,1)} copy(bf16[128,2048]{1,0:T(8,128)(2,1)S(1)} %copy-done.1) | data formatting | bytes 1048576
  54.6 0.4 copy-done
  55.0 0.0 copy-start.2
  55.0 0.8 %copy.15 = bf16[128,2048]{1,0:T(8,128)(2,1)} copy(bf16[128,2048]{1,0:T(8,128)(2,1)S(1)} %copy-done) | data formatting | bytes 1048576
  55.8 0.0 copy-done.2
  55.8 0.6 %copy.16 = f32[8,16]{1,0:T(8,128)} copy(f32[8,16]{1,0:T(8,128)S(1)} %copy-done.2) | data formatting | bytes 1024
Async XLA Ops:
  51.8 2.0 %copy-start.1 = (bf16[128,2048]{1,0:T(8,128)(2,1)S(1)}, bf16[128,2048]{1,0:T(8,128)(2,1)}, u32[]{:S(2)}) copy-start(bf16[128,2048]{1,0:T(8,128)(2,1)} %get-tuple-element.9) | copy-start | bytes 1572868
  53.8 1.2 %copy-start = (bf16[128,2048]{1,0:T(8,128)(2,1)S(1)}, bf16[128,2048]{1,0:T(8,128)(2,1)}, u32[]{:S(2)}) copy-start(bf16[128,2048]{1,0:T(8,128)(2,1)} %get-tuple-element.10) | copy-start | bytes 1572868
  55.0 0.8 %copy-start.2 = (f32[8,16]{1,0:T(8,128)S(1)}, f32[8,16]{1,0:T(8,128)}, u32[]{:S(2)}) copy-start(f32[8,16]{1,0:T(8,128)} %get-tuple-element.11) | copy-start | bytes 1540
